TPU v7x, 256 devices: a whole 4x4x8 slice. The times are simulated.
256 devices in a mesh: row: 4 (over x), col: 16 (over y, z_lo), gz: 4 (over z_hi, core).
Axes of the slice: x: 4, y: 4, z: 8 (z_hi: 2, z_lo: 4; z = z_hi * 4 + z_lo), core: 2. Of those that a mesh axis runs over, the one named last changes fastest.
Arguments:
- volume_field: bfloat16 [128, 32, 128, 512], P(None, 'row', 'col', 'gz'), may hold values from -6 to 6
- volume_load: bfloat16 [128, 32, 128, 512], P(None, 'row', 'col', 'gz'), may hold values from -6 to 6
- coefficient: float32 [32, 128, 512], P('row', 'col', 'gz'), may hold values from 0.25 to 2
- surface_block: bfloat16 [1024, 262144], P('row', 'col'), may hold values from -0.015625 to 0.015625
- trace_cell: int32 [4, 16, 4, 1024], P('row', 'col', 'gz'), may hold values from 0 to 8191, as said below
- flux_cell: int32 [4, 16, 4, 4], P('row', 'col', 'gz'), may hold values from 0 to 8191, as said below
Outputs:
- new_field: bfloat16 [128, 32, 128, 512], P(None, 'row', 'col', 'gz')
- surface_flux: float32 [128, 1024], P('gz', ('row', 'col'))
Inputs may be any that keep to these rules, and one draw needn't show every extreme that they name: `trace_cell`: within each device's 1024 entries, entry values are local cell numbers, one from each aligned run of 8 consecutive cells, in a permuted order; the first and last cells of the block are always chosen. `flux_cell`: within each device's 4 entries, entry values are local cell numbers, one from each aligned run of 2048 consecutive cells, in a permuted order; the first and last cells of the block are always chosen.
All inputs are finite; a program needn't handle non-finite values.
Results may differ from a plain program's by a relative error of at most 0.0032.
Values may be sent and summed in bfloat16 or wider, within the bound.
A program may use at most 128 MiB of HBM per device.

v0:
```python
import jax
import jax.numpy as jnp
from jax import lax
from jax.sharding import PartitionSpec as P

OMEGA = 0.8


def padded_2(array, sides, width):
    for axis, dim in sides:
        peers, length = (lax.axis_size(axis), array.shape[dim])
        up = [(i, (i + 1) % peers) for i in range(peers - 1)]
        down = [(j, i) for i, j in up]
        last = lax.slice_in_dim(array, length - width, length, axis=dim)
        first = lax.slice_in_dim(array, 0, width, axis=dim)
        before = lax.ppermute(last, axis, up)
        after = lax.ppermute(first, axis, down)
        array = jnp.concatenate([before, array, after], axis=dim)
    return array


def relax(current, source, diagonal):
    padded = padded_2(current, (("row", 1), ("col", 2), ("gz", 3)), 1).astype(jnp.float32)
    centre = current.astype(jnp.float32)
    beside = padded[:, 2:, 1:-1, 1:-1] + padded[:, :-2, 1:-1, 1:-1]
    beside = beside + padded[:, 1:-1, 2:, 1:-1] + padded[:, 1:-1, :-2, 1:-1]
    beside = beside + padded[:, 1:-1, 1:-1, 2:] + padded[:, 1:-1, 1:-1, :-2]
    return (centre + OMEGA * (source - (diagonal * centre - beside)) / diagonal).astype(
        jnp.bfloat16
    )


def per_device(volume_field, volume_load, coefficient, surface_block, trace_cell, flux_cell):
    side_count, first_span, second_span, third_span = volume_field.shape
    cell_count = first_span * second_span * third_span
    slot_count = trace_cell.shape[3]
    flux_slots = flux_cell.shape[3]
    side_group = side_count // lax.axis_size("gz")
    flat_field = volume_field.reshape(side_count, cell_count)
    picker = (
        lax.broadcasted_iota(jnp.int32, (cell_count, slot_count), 0)
        == trace_cell.reshape(1, slot_count)
    ).astype(jnp.bfloat16)
    trace_values = jnp.dot(flat_field, picker, preferred_element_type=jnp.float32).astype(
        jnp.bfloat16
    )
    layer_index = lax.axis_index("gz")
    chosen = lax.dynamic_slice_in_dim(
        lax.all_gather(trace_values, ("row", "gz"), axis=1, tiled=True),
        layer_index * side_group,
        side_group,
        0,
    )
    partial_flux = lax.dot_general(
        chosen, surface_block, (((1,), (1,)), ((), ())), preferred_element_type=jnp.float32
    )
    surface_flux = lax.psum_scatter(partial_flux, "col", scatter_dimension=1, tiled=True)
    owned_flux = lax.all_to_all(surface_flux, "gz", split_axis=1, concat_axis=0, tiled=True)
    placer = (
        flux_cell.reshape(flux_slots, 1)
        == lax.broadcasted_iota(jnp.int32, (flux_slots, cell_count), 1)
    ).astype(jnp.float32)
    placed = jnp.dot(
        owned_flux, placer, precision=lax.Precision.HIGHEST, preferred_element_type=jnp.float32
    )
    source = volume_load.astype(jnp.float32) + placed.reshape(
        side_count, first_span, second_span, third_span
    )
    diagonal = 6.0 + coefficient
    current = volume_field
    for repeat in range(3):
        current = relax(current, source, diagonal)
    return (current, surface_flux)


def solution(mesh):
    in_specs = (
        P(None, "row", "col", "gz"),
        P(None, "row", "col", "gz"),
        P("row", "col", "gz"),
        P("row", "col"),
        P("row", "col", "gz", None),
        P("row", "col", "gz", None),
    )
    out_specs = (P(None, "row", "col", "gz"), P("gz", ("row", "col")))
    return jax.shard_map(
        per_device, mesh=mesh, in_specs=in_specs, out_specs=out_specs, check_vma=False
    )
```

profile of v0, /device:TPU:17, one launch (start us, length us, event | category | flops | bytes accessed | tf_op | source)
XLA Modules:
  0.0 316.4 jit_solution(1257853080280869536)
XLA Ops:
  7.2 8.3 %fusion.22 = bf16[128,1024]{1,0:T(8,128)(2,1)} fusion(bf16[16,8,64,128]{3,2,1,0:T(8,128)(2,1)} %bitcast.27, s32[1024]{0:T(1024)} %bitcast.29), kind=kOutput, calls=%fused_computation.46 | convolution fusion | flops 2156003328 | bytes 2363392 | tf_op jit(solution)/shard_map/dot_general | solution.py:44
  15.6 3.3 %copy.15 = bf16[128,8,8,128]{0,3,2,1:T(8,128)(2,1)S(1)} copy(bf16[128,8,8,128]{3,2,1,0:T(8,128)(2,1)} %param.6) | data formatting | bytes 4194304 | tf_op args[0]
  19.0 3.1 collective-permute-start
  23.4 3.7 %collective-permute-done = bf16[128,1,8,128]{0,3,2,1:T(8,128)(2,1)S(1)} collective-permute-done((bf16[128,1,8,128]{0,3,2,1:T(8,128)(2,1)S(1)}, bf16[128,1,8,128]{0,3,2,1:T(8,128)(2,1)S(1)}, u32[]{:S(2)}, u32[]{:S(2)}) %collective-permute-start) | collective-permute-done | bytes 262176 | tf_op jit(solution)/shard_map/ppermute | solution.py:16
  27.1 3.8 %collective-permute-done.1 = bf16[128,1,8,128]{0,3,2,1:T(8,128)(2,1)S(1)} collective-permute-done((bf16[128,1,8,128]{0,3,2,1:T(8,128)(2,1)S(1)}, bf16[128,1,8,128]{0,3,2,1:T(8,128)(2,1)S(1)}, u32[]{:S(2)}, u32[]{:S(2)}) %collective-permute-start.1) | collective-permute-done | bytes 262176 | tf_op jit(solution)/shard_map/ppermute | solution.py:17
  31.8 3.5 %collective-permute-start.2 = (bf16[128,10,1,128]{0,3,2,1:T(8,128)(2,1)}, bf16[128,10,1,128]{0,3,2,1:T(8,128)(2,1)S(1)}, u32[]{:S(2)}, u32[]{:S(2)}) collective-permute-start(bf16[128,10,1,128]{0,3,2,1:T(8,128)(2,1)} %get-tuple-element.16), channel_id=1, source_target_pairs={{0,4},{4,8},{8,12},{12,16},{16,20},{20,24},{24,28},{28,32},{32,36}... | collective-permute-start | bytes 983048 | tf_op jit(solution)/shard_map/ppermute | solution.py:16
  35.4 4.5 %collective-permute-start.3 = (bf16[128,10,1,128]{0,3,2,1:T(8,128)(2,1)}, bf16[128,10,1,128]{0,3,2,1:T(8,128)(2,1)S(1)}, u32[]{:S(2)}, u32[]{:S(2)}) collective-permute-start(bf16[128,10,1,128]{0,3,2,1:T(8,128)(2,1)} %get-tuple-element.17), channel_id=1, source_target_pairs={{4,0},{8,4},{12,8},{16,12},{20,16},{24,20},{28,24},{32,28},{36,32}... | collective-permute-start | bytes 983048 | tf_op jit(solution)/shard_map/ppermute | solution.py:17
  39.9 8.5 %collective-permute-done.2 = bf16[128,10,1,128]{0,3,2,1:T(8,128)(2,1)S(1)} collective-permute-done((bf16[128,10,1,128]{0,3,2,1:T(8,128)(2,1)}, bf16[128,10,1,128]{0,3,2,1:T(8,128)(2,1)S(1)}, u32[]{:S(2)}, u32[]{:S(2)}) %collective-permute-start.2) | collective-permute-done | bytes 327712 | tf_op jit(solution)/shard_map/ppermute | solution.py:16
  48.5 5.0 %collective-permute-done.3 = bf16[128,10,1,128]{0,3,2,1:T(8,128)(2,1)S(1)} collective-permute-done((bf16[128,10,1,128]{0,3,2,1:T(8,128)(2,1)}, bf16[128,10,1,128]{0,3,2,1:T(8,128)(2,1)S(1)}, u32[]{:S(2)}, u32[]{:S(2)}) %collective-permute-start.3) | collective-permute-done | bytes 327712 | tf_op jit(solution)/shard_map/ppermute | solution.py:17
  53.6 8.9 %collective-permute-start.4 = (bf16[128,10,10,1]{0,3,2,1:T(2,128)(2,1)S(1)}, bf16[128,10,10,1]{0,3,2,1:T(2,128)(2,1)S(1)}, u32[]{:S(2)}, u32[]{:S(2)}) collective-permute-start(bf16[128,10,10,1]{0,3,2,1:T(2,128)(2,1)S(1)} %get-tuple-element.10), channel_id=1, source_target_pairs={{0,1},{1,2},{2,3},{4,5},{5,6},{6,7},{8,9},{9,10},{10,11},{12,13},{... | collective-permute-start | bytes 76808 | tf_op jit(solution)/shard_map/ppermute | solution.py:16
  64.4 32.9 %all-gather.2.cloned.1.call-done = bf16[128,16384]{1,0:T(8,128)(2,1)} async-done(((bf16[128,1024]{1,0:T(8,128)(2,1)}), bf16[128,16384]{1,0:T(8,128)(2,1)}) %all-gather.2.cloned.1.call-update) | async-done | bytes 4194320 | tf_op jit(solution)/shard_map/all_gather | solution.py:49
  97.4 6.7 %fusion.25 = f32[32,256]{0,1:T(8,128)} fusion(bf16[256,16384]{1,0:T(8,128)(2,1)} %param.9, bf16[128,16384]{1,0:T(8,128)(2,1)} %all-gather.2.cloned.1.call-done, s32[]{:T(128)S(6)} %select_n.3), kind=kOutput, calls=%fused_computation.47 | convolution fusion | flops 268435456 | bytes 9469956 | tf_op jit(solution)/shard_map/dot_general | solution.py:54
  104.1 4.2 %copy.16 = bf16[128,8,8,128]{0,3,2,1:T(8,128)(2,1)} copy(bf16[128,8,8,128]{3,2,1,0:T(8,128)(2,1)} %param.7) | data formatting | bytes 4194304 | tf_op args[1]
  108.3 53.4 %reduce-scatter.2.cloned.1.call-done = f32[32,16]{0,1:T(8,128)} async-done(((f32[32,256]{0,1:T(8,128)}), f32[32,16]{0,1:T(8,128)}) %reduce-scatter.2.cloned.1.call-update) | async-done | bytes 2064 | tf_op jit(solution)/shard_map/reduce_scatter | solution.py:57
  163.1 17.1 %all-to-all-start = ((f32[4,1,128]{2,1,0:T(1,128)}), f32[4,1,128]{2,1,0:T(1,128)}, u32[]{:S(2)}, u32[]{:S(2)}) async-start(f32[4,1,128]{2,1,0:T(1,128)} %reshape.41), calls=%async_computation.1 | async-start | bytes 4096 | tf_op jit(solution)/shard_map/all_to_all | solution.py:58
  180.1 4.7 %maximum_convert_fusion = f32[128,10,10,130]{0,3,2,1:T(8,128)} fusion(bf16[128,10,10,1]{0,3,2,1:T(2,128)(2,1)S(1)} %collective-permute-done.5, bf16[128,10,1,128]{0,3,2,1:T(8,128)(2,1)S(1)} %collective-permute-done.3, bf16[128,1,8,128]{0,3,2,1:T(8,128)(2,1)S(1)} %collective-permute-done.1, bf16[128,8,8,128]{0,3,2,1:T(8,128)(2,1)S(1)} %copy.15, ...), kind=kLoop, calls=%fused_computation.40 | loop fusion | flops 23296000 | bytes 9984000 | tf_op jit(solution)/shard_map/convert_element_type | solution.py:23
  188.8 14.0 %fusion.14 = (bf16[128,8,8,128]{0,3,2,1:T(8,128)(2,1)S(1)}, f32[128,8,8,128]{0,3,2,1:T(8,128)}) fusion(f32[128,10,10,130]{0,3,2,1:T(8,128)} %maximum_convert_fusion, bf16[128,8,8,128]{0,3,2,1:T(8,128)(2,1)S(1)} %copy.15, f32[8,8,128]{2,1,0:T(8,128)S(1)} %broadcast_add_fusion, s32[8,8,128]{2,1,0:T(8,128)S(1)} %multiply_add_fusion, s32[4]{0:T(128)S(1)} %bitcast.30, ...), kind=kOutput, calls=%fused_computation.37 | convolution fusion | flops 66093056 | bytes 35719184 | tf_op jit(solution)/shard_map/dot_general | solution.py:63
  207.1 3.3 %collective-permute-done.6 = bf16[128,1,8,128]{0,3,2,1:T(8,128)(2,1)S(1)} collective-permute-done((bf16[128,1,8,128]{0,3,2,1:T(8,128)(2,1)S(1)}, bf16[128,1,8,128]{0,3,2,1:T(8,128)(2,1)S(1)}, u32[]{:S(2)}, u32[]{:S(2)}) %collective-permute-start.6) | collective-permute-done | bytes 262176 | tf_op jit(solution)/shard_map/ppermute | solution.py:16
  210.4 3.8 %collective-permute-done.7 = bf16[128,1,8,128]{0,3,2,1:T(8,128)(2,1)S(1)} collective-permute-done((bf16[128,1,8,128]{0,3,2,1:T(8,128)(2,1)S(1)}, bf16[128,1,8,128]{0,3,2,1:T(8,128)(2,1)S(1)}, u32[]{:S(2)}, u32[]{:S(2)}) %collective-permute-start.7) | collective-permute-done | bytes 262176 | tf_op jit(solution)/shard_map/ppermute | solution.py:17
  217.2 5.1 %collective-permute-start.9 = (bf16[128,10,1,128]{0,3,2,1:T(8,128)(2,1)S(1)}, bf16[128,10,1,128]{0,3,2,1:T(8,128)(2,1)S(1)}, u32[]{:S(2)}, u32[]{:S(2)}) collective-permute-start(bf16[128,10,1,128]{0,3,2,1:T(8,128)(2,1)S(1)} %get-tuple-element.15), channel_id=1, source_target_pairs={{4,0},{8,4},{12,8},{16,12},{20,16},{24,20},{28,24},{32,28},{36,32}... | collective-permute-start | bytes 983048 | tf_op jit(solution)/shard_map/ppermute | solution.py:17
  222.4 3.8 %collective-permute-done.8 = bf16[128,10,1,128]{0,3,2,1:T(8,128)(2,1)S(1)} collective-permute-done((bf16[128,10,1,128]{0,3,2,1:T(8,128)(2,1)S(1)}, bf16[128,10,1,128]{0,3,2,1:T(8,128)(2,1)S(1)}, u32[]{:S(2)}, u32[]{:S(2)}) %collective-permute-start.8) | collective-permute-done | bytes 327712 | tf_op jit(solution)/shard_map/ppermute | solution.py:16
  226.1 6.6 %collective-permute-done.9 = bf16[128,10,1,128]{0,3,2,1:T(8,128)(2,1)S(1)} collective-permute-done((bf16[128,10,1,128]{0,3,2,1:T(8,128)(2,1)S(1)}, bf16[128,10,1,128]{0,3,2,1:T(8,128)(2,1)S(1)}, u32[]{:S(2)}, u32[]{:S(2)}) %collective-permute-start.9) | collective-permute-done | bytes 327712 | tf_op jit(solution)/shard_map/ppermute | solution.py:17
  232.8 9.6 %collective-permute-start.10 = (bf16[128,10,10,1]{0,3,2,1:T(2,128)(2,1)S(1)}, bf16[128,10,10,1]{0,3,2,1:T(2,128)(2,1)S(1)}, u32[]{:S(2)}, u32[]{:S(2)}) collective-permute-start(bf16[128,10,10,1]{0,3,2,1:T(2,128)(2,1)S(1)} %get-tuple-element.8), channel_id=1, source_target_pairs={{0,1},{1,2},{2,3},{4,5},{5,6},{6,7},{8,9},{9,10},{10,11},{12,13},{... | collective-permute-start | bytes 76808 | tf_op jit(solution)/shard_map/ppermute | solution.py:16
  244.7 7.4 %collective-permute-done.11 = bf16[128,10,10,1]{0,3,2,1:T(2,128)(2,1)S(1)} collective-permute-done((bf16[128,10,10,1]{0,3,2,1:T(2,128)(2,1)S(1)}, bf16[128,10,10,1]{0,3,2,1:T(2,128)(2,1)S(1)}, u32[]{:S(2)}, u32[]{:S(2)}) %collective-permute-start.11) | collective-permute-done | bytes 25632 | tf_op jit(solution)/shard_map/ppermute | solution.py:17
  255.1 4.5 %fusion.15 = bf16[128,8,8,128]{0,3,2,1:T(8,128)(2,1)S(1)} fusion(f32[128,8,8,128]{0,3,2,1:T(8,128)S(1)} %copy-done, f32[128,10,10,130]{0,3,2,1:T(8,128)S(1)} %maximum_convert_fusion.1, bf16[128,8,8,128]{0,3,2,1:T(8,128)(2,1)S(1)} %get-tuple-element.24, f32[8,8,128]{2,1,0:T(8,128)S(1)} %broadcast_add_fusion), kind=kLoop, calls=%fused_computation.38 | loop fusion | flops 13631488 | bytes 33587200 | tf_op jit(solution)/shard_map/convert_element_type | solution.py:28
  266.0 3.8 %collective-permute-done.13 = bf16[128,1,8,128]{0,3,2,1:T(8,128)(2,1)S(1)} collective-permute-done((bf16[128,1,8,128]{0,3,2,1:T(8,128)(2,1)S(1)}, bf16[128,1,8,128]{0,3,2,1:T(8,128)(2,1)S(1)}, u32[]{:S(2)}, u32[]{:S(2)}) %collective-permute-start.13) | collective-permute-done | bytes 262176 | tf_op jit(solution)/shard_map/ppermute | solution.py:17
  270.0 4.6 %collective-permute-start.14 = (bf16[128,10,1,128]{0,3,2,1:T(8,128)(2,1)S(1)}, bf16[128,10,1,128]{0,3,2,1:T(8,128)(2,1)S(1)}, u32[]{:S(2)}, u32[]{:S(2)}) collective-permute-start(bf16[128,10,1,128]{0,3,2,1:T(8,128)(2,1)S(1)} %get-tuple-element.12), channel_id=1, source_target_pairs={{0,4},{4,8},{8,12},{12,16},{16,20},{20,24},{24,28},{28,32},{32,36}... | collective-permute-start | bytes 983048 | tf_op jit(solution)/shard_map/ppermute | solution.py:16
  274.5 3.4 %collective-permute-start.15 = (bf16[128,10,1,128]{0,3,2,1:T(8,128)(2,1)S(1)}, bf16[128,10,1,128]{0,3,2,1:T(8,128)(2,1)S(1)}, u32[]{:S(2)}, u32[]{:S(2)}) collective-permute-start(bf16[128,10,1,128]{0,3,2,1:T(8,128)(2,1)S(1)} %get-tuple-element.13), channel_id=1, source_target_pairs={{4,0},{8,4},{12,8},{16,12},{20,16},{24,20},{28,24},{32,28},{36,32}... | collective-permute-start | bytes 983048 | tf_op jit(solution)/shard_map/ppermute | solution.py:17
  278.0 5.4 %collective-permute-done.14 = bf16[128,10,1,128]{0,3,2,1:T(8,128)(2,1)S(1)} collective-permute-done((bf16[128,10,1,128]{0,3,2,1:T(8,128)(2,1)S(1)}, bf16[128,10,1,128]{0,3,2,1:T(8,128)(2,1)S(1)}, u32[]{:S(2)}, u32[]{:S(2)}) %collective-permute-start.14) | collective-permute-done | bytes 327712 | tf_op jit(solution)/shard_map/ppermute | solution.py:16
  283.3 4.6 %collective-permute-done.15 = bf16[128,10,1,128]{0,3,2,1:T(8,128)(2,1)S(1)} collective-permute-done((bf16[128,10,1,128]{0,3,2,1:T(8,128)(2,1)S(1)}, bf16[128,10,1,128]{0,3,2,1:T(8,128)(2,1)S(1)}, u32[]{:S(2)}, u32[]{:S(2)}) %collective-permute-start.15) | collective-permute-done | bytes 327712 | tf_op jit(solution)/shard_map/ppermute | solution.py:17
  292.3 6.9 %collective-permute-done.17 = bf16[128,10,10,1]{0,3,2,1:T(2,128)(2,1)S(1)} collective-permute-done((bf16[128,10,10,1]{0,3,2,1:T(2,128)(2,1)S(1)}, bf16[128,10,10,1]{0,3,2,1:T(2,128)(2,1)S(1)}, u32[]{:S(2)}, u32[]{:S(2)}) %collective-permute-start.17) | collective-permute-done | bytes 25632 | tf_op jit(solution)/shard_map/ppermute | solution.py:17
  302.2 4.5 %fusion.16 = bf16[128,8,8,128]{0,3,2,1:T(8,128)(2,1)S(1)} fusion(f32[128,8,8,128]{0,3,2,1:T(8,128)S(1)} %copy-done, f32[128,10,10,130]{0,3,2,1:T(8,128)S(1)} %maximum_convert_fusion.2, bf16[128,8,8,128]{0,3,2,1:T(8,128)(2,1)S(1)} %fusion.15, f32[8,8,128]{2,1,0:T(8,128)S(1)} %broadcast_add_fusion), kind=kLoop, calls=%fused_computation.39 | loop fusion | flops 13631488 | bytes 33587200 | tf_op jit(solution)/shard_map/convert_element_type | solution.py:28
  (47 shorter events, 38.8 us)
Async XLA Ops:
  7.2 90.2 %all-gather.2.cloned.1.call-start = ((), (), s32[]{:S(2)}) async-start(), calls=%async_computation.2 | async-start | bytes 4456448 | tf_op jit(solution)/shard_map/all_gather | solution.py:49
  15.5 24.4 %copy-start.1 = (f32[8,8,128]{2,1,0:T(8,128)S(1)}, f32[8,8,128]{2,1,0:T(8,128)}, u32[]{:S(2)}) copy-start(f32[8,8,128]{2,1,0:T(8,128)} %param.8) | copy-start | bytes 98308
  15.6 146.1 %reduce-scatter.2.cloned.1.call-start = ((), (), s32[]{:S(2)}) async-start(), calls=%async_computation.3 | async-start | bytes 139264 | tf_op jit(solution)/shard_map/reduce_scatter | solution.py:57
  19.0 8.1 %collective-permute-start = (bf16[128,1,8,128]{0,3,2,1:T(8,128)(2,1)S(1)}, bf16[128,1,8,128]{0,3,2,1:T(8,128)(2,1)S(1)}, u32[]{:S(2)}, u32[]{:S(2)}) collective-permute-start(bf16[128,1,8,128]{0,3,2,1:T(8,128)(2,1)S(1)} %get-tuple-element.22), channel_id=1, source_target_pairs={{0,64},{64,128},{128,192},{1,65},{65,129},{129,193},{2,66},{66,130... | collective-permute-start | bytes 786440 | tf_op jit(solution)/shard_map/ppermute | solution.py:16
  22.1 8.8 %collective-permute-start.1 = (bf16[128,1,8,128]{0,3,2,1:T(8,128)(2,1)S(1)}, bf16[128,1,8,128]{0,3,2,1:T(8,128)(2,1)S(1)}, u32[]{:S(2)}, u32[]{:S(2)}) collective-permute-start(bf16[128,1,8,128]{0,3,2,1:T(8,128)(2,1)S(1)} %get-tuple-element.23), channel_id=1, source_target_pairs={{64,0},{128,64},{192,128},{65,1},{129,65},{193,129},{66,2},{130,66... | collective-permute-start | bytes 786440 | tf_op jit(solution)/shard_map/ppermute | solution.py:17
  31.8 16.6 %collective-permute-start.2 = (bf16[128,10,1,128]{0,3,2,1:T(8,128)(2,1)}, bf16[128,10,1,128]{0,3,2,1:T(8,128)(2,1)S(1)}, u32[]{:S(2)}, u32[]{:S(2)}) collective-permute-start(bf16[128,10,1,128]{0,3,2,1:T(8,128)(2,1)} %get-tuple-element.16), channel_id=1, source_target_pairs={{0,4},{4,8},{8,12},{12,16},{16,20},{20,24},{24,28},{28,32},{32,36}... | collective-permute-start | bytes 983048 | tf_op jit(solution)/shard_map/ppermute | solution.py:16
  35.4 18.1 %collective-permute-start.3 = (bf16[128,10,1,128]{0,3,2,1:T(8,128)(2,1)}, bf16[128,10,1,128]{0,3,2,1:T(8,128)(2,1)S(1)}, u32[]{:S(2)}, u32[]{:S(2)}) collective-permute-start(bf16[128,10,1,128]{0,3,2,1:T(8,128)(2,1)} %get-tuple-element.17), channel_id=1, source_target_pairs={{4,0},{8,4},{12,8},{16,12},{20,16},{24,20},{28,24},{32,28},{36,32}... | collective-permute-start | bytes 983048 | tf_op jit(solution)/shard_map/ppermute | solution.py:17
  53.6 126.6 %collective-permute-start.4 = (bf16[128,10,10,1]{0,3,2,1:T(2,128)(2,1)S(1)}, bf16[128,10,10,1]{0,3,2,1:T(2,128)(2,1)S(1)}, u32[]{:S(2)}, u32[]{:S(2)}) collective-permute-start(bf16[128,10,10,1]{0,3,2,1:T(2,128)(2,1)S(1)} %get-tuple-element.10), channel_id=1, source_target_pairs={{0,1},{1,2},{2,3},{4,5},{5,6},{6,7},{8,9},{9,10},{10,11},{12,13},{... | collective-permute-start | bytes 76808 | tf_op jit(solution)/shard_map/ppermute | solution.py:16
  62.5 117.6 %collective-permute-start.5 = (bf16[128,10,10,1]{0,3,2,1:T(2,128)(2,1)S(1)}, bf16[128,10,10,1]{0,3,2,1:T(2,128)(2,1)S(1)}, u32[]{:S(2)}, u32[]{:S(2)}) collective-permute-start(bf16[128,10,10,1]{0,3,2,1:T(2,128)(2,1)S(1)} %get-tuple-element.11), channel_id=1, source_target_pairs={{1,0},{2,1},{3,2},{5,4},{6,5},{7,6},{9,8},{10,9},{11,10},{13,12},{... | collective-permute-start | bytes 76808 | tf_op jit(solution)/shard_map/ppermute | solution.py:17
  163.1 23.9 %all-to-all-start = ((f32[4,1,128]{2,1,0:T(1,128)}), f32[4,1,128]{2,1,0:T(1,128)}, u32[]{:S(2)}, u32[]{:S(2)}) async-start(f32[4,1,128]{2,1,0:T(1,128)} %reshape.41), calls=%async_computation.1 | async-start | bytes 4096 | tf_op jit(solution)/shard_map/all_to_all | solution.py:58
  180.1 8.7 %copy-start.2 = (s32[1,1,1,4]{3,2,1,0:T(1,128)S(1)}, s32[1,1,1,4]{3,2,1,0:T(1,128)}, u32[]{:S(2)}) copy-start(s32[1,1,1,4]{3,2,1,0:T(1,128)} %param.11) | copy-start | bytes 52
  202.8 7.6 %collective-permute-start.6 = (bf16[128,1,8,128]{0,3,2,1:T(8,128)(2,1)S(1)}, bf16[128,1,8,128]{0,3,2,1:T(8,128)(2,1)S(1)}, u32[]{:S(2)}, u32[]{:S(2)}) collective-permute-start(bf16[128,1,8,128]{0,3,2,1:T(8,128)(2,1)S(1)} %get-tuple-element.20), channel_id=1, source_target_pairs={{0,64},{64,128},{128,192},{1,65},{65,129},{129,193},{2,66},{66,130... | collective-permute-start | bytes 786440 | tf_op jit(solution)/shard_map/ppermute | solution.py:16
  205.8 8.5 %collective-permute-start.7 = (bf16[128,1,8,128]{0,3,2,1:T(8,128)(2,1)S(1)}, bf16[128,1,8,128]{0,3,2,1:T(8,128)(2,1)S(1)}, u32[]{:S(2)}, u32[]{:S(2)}) collective-permute-start(bf16[128,1,8,128]{0,3,2,1:T(8,128)(2,1)S(1)} %get-tuple-element.21), channel_id=1, source_target_pairs={{64,0},{128,64},{192,128},{65,1},{129,65},{193,129},{66,2},{130,66... | collective-permute-start | bytes 786440 | tf_op jit(solution)/shard_map/ppermute | solution.py:17
  214.4 11.8 %collective-permute-start.8 = (bf16[128,10,1,128]{0,3,2,1:T(8,128)(2,1)S(1)}, bf16[128,10,1,128]{0,3,2,1:T(8,128)(2,1)S(1)}, u32[]{:S(2)}, u32[]{:S(2)}) collective-permute-start(bf16[128,10,1,128]{0,3,2,1:T(8,128)(2,1)S(1)} %get-tuple-element.14), channel_id=1, source_target_pairs={{0,4},{4,8},{8,12},{12,16},{16,20},{20,24},{24,28},{28,32},{32,36}... | collective-permute-start | bytes 983048 | tf_op jit(solution)/shard_map/ppermute | solution.py:16
  217.2 15.5 %collective-permute-start.9 = (bf16[128,10,1,128]{0,3,2,1:T(8,128)(2,1)S(1)}, bf16[128,10,1,128]{0,3,2,1:T(8,128)(2,1)S(1)}, u32[]{:S(2)}, u32[]{:S(2)}) collective-permute-start(bf16[128,10,1,128]{0,3,2,1:T(8,128)(2,1)S(1)} %get-tuple-element.15), channel_id=1, source_target_pairs={{4,0},{8,4},{12,8},{16,12},{20,16},{24,20},{28,24},{32,28},{36,32}... | collective-permute-start | bytes 983048 | tf_op jit(solution)/shard_map/ppermute | solution.py:17
  232.8 11.9 %collective-permute-start.10 = (bf16[128,10,10,1]{0,3,2,1:T(2,128)(2,1)S(1)}, bf16[128,10,10,1]{0,3,2,1:T(2,128)(2,1)S(1)}, u32[]{:S(2)}, u32[]{:S(2)}) collective-permute-start(bf16[128,10,10,1]{0,3,2,1:T(2,128)(2,1)S(1)} %get-tuple-element.8), channel_id=1, source_target_pairs={{0,1},{1,2},{2,3},{4,5},{5,6},{6,7},{8,9},{9,10},{10,11},{12,13},{... | collective-permute-start | bytes 76808 | tf_op jit(solution)/shard_map/ppermute | solution.py:16
  242.5 12.6 %copy-start = (f32[128,8,8,128]{0,3,2,1:T(8,128)S(1)}, f32[128,8,8,128]{0,3,2,1:T(8,128)}, u32[]{:S(2)}) copy-start(f32[128,8,8,128]{0,3,2,1:T(8,128)} %get-tuple-element.25) | copy-start | bytes 12582916
  242.5 9.6 %collective-permute-start.11 = (bf16[128,10,10,1]{0,3,2,1:T(2,128)(2,1)S(1)}, bf16[128,10,10,1]{0,3,2,1:T(2,128)(2,1)S(1)}, u32[]{:S(2)}, u32[]{:S(2)}) collective-permute-start(bf16[128,10,10,1]{0,3,2,1:T(2,128)(2,1)S(1)} %get-tuple-element.9), channel_id=1, source_target_pairs={{1,0},{2,1},{3,2},{5,4},{6,5},{7,6},{9,8},{10,9},{11,10},{13,12},{... | collective-permute-start | bytes 76808 | tf_op jit(solution)/shard_map/ppermute | solution.py:17
  259.7 6.4 %collective-permute-start.12 = (bf16[128,1,8,128]{0,3,2,1:T(8,128)(2,1)S(1)}, bf16[128,1,8,128]{0,3,2,1:T(8,128)(2,1)S(1)}, u32[]{:S(2)}, u32[]{:S(2)}) collective-permute-start(bf16[128,1,8,128]{0,3,2,1:T(8,128)(2,1)S(1)} %get-tuple-element.18), channel_id=1, source_target_pairs={{0,64},{64,128},{128,192},{1,65},{65,129},{129,193},{2,66},{66,130... | collective-permute-start | bytes 786440 | tf_op jit(solution)/shard_map/ppermute | solution.py:16
  262.8 7.1 %collective-permute-start.13 = (bf16[128,1,8,128]{0,3,2,1:T(8,128)(2,1)S(1)}, bf16[128,1,8,128]{0,3,2,1:T(8,128)(2,1)S(1)}, u32[]{:S(2)}, u32[]{:S(2)}) collective-permute-start(bf16[128,1,8,128]{0,3,2,1:T(8,128)(2,1)S(1)} %get-tuple-element.19), channel_id=1, source_target_pairs={{64,0},{128,64},{192,128},{65,1},{129,65},{193,129},{66,2},{130,66... | collective-permute-start | bytes 786440 | tf_op jit(solution)/shard_map/ppermute | solution.py:17
  270.0 13.4 %collective-permute-start.14 = (bf16[128,10,1,128]{0,3,2,1:T(8,128)(2,1)S(1)}, bf16[128,10,1,128]{0,3,2,1:T(8,128)(2,1)S(1)}, u32[]{:S(2)}, u32[]{:S(2)}) collective-permute-start(bf16[128,10,1,128]{0,3,2,1:T(8,128)(2,1)S(1)} %get-tuple-element.12), channel_id=1, source_target_pairs={{0,4},{4,8},{8,12},{12,16},{16,20},{20,24},{24,28},{28,32},{32,36}... | collective-permute-start | bytes 983048 | tf_op jit(solution)/shard_map/ppermute | solution.py:16
  274.5 13.4 %collective-permute-start.15 = (bf16[128,10,1,128]{0,3,2,1:T(8,128)(2,1)S(1)}, bf16[128,10,1,128]{0,3,2,1:T(8,128)(2,1)S(1)}, u32[]{:S(2)}, u32[]{:S(2)}) collective-permute-start(bf16[128,10,1,128]{0,3,2,1:T(8,128)(2,1)S(1)} %get-tuple-element.13), channel_id=1, source_target_pairs={{4,0},{8,4},{12,8},{16,12},{20,16},{24,20},{28,24},{32,28},{36,32}... | collective-permute-start | bytes 983048 | tf_op jit(solution)/shard_map/ppermute | solution.py:17
  288.0 4.3 %collective-permute-start.16 = (bf16[128,10,10,1]{0,3,2,1:T(2,128)(2,1)S(1)}, bf16[128,10,10,1]{0,3,2,1:T(2,128)(2,1)S(1)}, u32[]{:S(2)}, u32[]{:S(2)}) collective-permute-start(bf16[128,10,10,1]{0,3,2,1:T(2,128)(2,1)S(1)} %get-tuple-element.6), channel_id=1, source_target_pairs={{0,1},{1,2},{2,3},{4,5},{5,6},{6,7},{8,9},{9,10},{10,11},{12,13},{... | collective-permute-start | bytes 76808 | tf_op jit(solution)/shard_map/ppermute | solution.py:16
  289.9 9.3 %collective-permute-start.17 = (bf16[128,10,10,1]{0,3,2,1:T(2,128)(2,1)S(1)}, bf16[128,10,10,1]{0,3,2,1:T(2,128)(2,1)S(1)}, u32[]{:S(2)}, u32[]{:S(2)}) collective-permute-start(bf16[128,10,10,1]{0,3,2,1:T(2,128)(2,1)S(1)} %get-tuple-element.7), channel_id=1, source_target_pairs={{1,0},{2,1},{3,2},{5,4},{6,5},{7,6},{9,8},{10,9},{11,10},{13,12},{... | collective-permute-start | bytes 76808 | tf_op jit(solution)/shard_map/ppermute | solution.py:17
Sparse Core Ops, SparseCore 0:
  15.7 81.6 all-gather.1
  104.2 57.4 reduce-scatter.1
where the time goes:
time: 317 us; the launch traced here: 316 us
  waiting for transfers between devices  157 us (50%)
  starting transfers between devices  81.2 us (26%)
  matrix products  28.9 us (9%)
  other arithmetic  22.3 us (7%)
  between operations  14.3 us (5%)
  local copies, waits for them, and re-layouts  12.4 us (4%)
    reduce_scatter x1, waiting for transfers between devices, per_device(): lax.psum_scatter(partial_flux, 'col', scatter_dimension=1, tiled=True)  53.4 us
    ppermute x9, waiting for transfers between devices, padded_2(): after = lax.ppermute(first, axis, down)  42 us
    ppermute x9, starting transfers between devices, padded_2(): before = lax.ppermute(last, axis, up)  40.6 us
    all_gather x1, waiting for transfers between devices, per_device(): lax.all_gather(trace_values, ('row', 'gz'), axis=1, tiled=True)  32.9 us
    ppermute x9, waiting for transfers between devices, padded_2(): before = lax.ppermute(last, axis, up)  26.7 us
    ppermute x9, starting transfers between devices, padded_2(): after = lax.ppermute(first, axis, down)  23.4 us
    all_to_all x1, starting transfers between devices, per_device(): lax.all_to_all(surface_flux, 'gz', split_axis=1, concat_axis=0, tiled=True)  17.1 us
    dot_general x1, matrix products, per_device(): jnp.dot(owned_flux, placer, precision=lax.Precision.HIGHEST, preferred_el...  14 us
  transfers between devices with their start and end apart: 21, of which 17 were waited for; matrix products, arithmetic and copies ran while one was open for 7% of the time, Pallas kernels for 0%

commit v1 on v0

--- a/solution.py
+++ b/solution.py
@@ -55,7 +55,10 @@
         chosen, surface_block, (((1,), (1,)), ((), ())), preferred_element_type=jnp.float32
     )
     surface_flux = lax.psum_scatter(partial_flux, "col", scatter_dimension=1, tiled=True)
-    owned_flux = lax.all_to_all(surface_flux, "gz", split_axis=1, concat_axis=0, tiled=True)
+    owned_flux = jnp.concatenate(
+        lax.all_to_all(jnp.stack(jnp.split(surface_flux, lax.axis_size("gz"), axis=1)), "gz", 0, 0),
+        axis=0,
+    )
     placer = (
         flux_cell.reshape(flux_slots, 1)
         == lax.broadcasted_iota(jnp.int32, (flux_slots, cell_count), 1)

time: 317 us -> 316 us (level)
  starting transfers between devices: 81.2 us -> 72.8 us
  waiting for transfers between devices: 157 us -> 164 us
    all_gather x1, waiting for transfers between devices: 32.9 us -> 56.3 us  [per_device(): lax.all_gather(trace_values, ('row', 'gz'), axis=1, tiled=True)]
    ppermute x9, waiting for transfers between devices: 26.7 us -> 15.4 us  [padded_2(): before = lax.ppermute(last, axis, up)]
    ppermute x9, starting transfers between devices: 40.6 us -> 31.7 us  [padded_2(): before = lax.ppermute(last, axis, up)]
    ppermute x9, waiting for transfers between devices: 42 us -> 36.6 us  [padded_2(): after = lax.ppermute(first, axis, down)]
    unnamed x11 -> x13, local copies, waits for them, and re-layouts: 11.7 us -> 11 us
  transfers between devices with their start and end apart: 21 -> 21, of which waited for: 17 -> 14; matrix products, arithmetic and copies ran while one was open for 7% -> 7% of each run, Pallas kernels for 0% -> 0%
where the time goes in v1:
time: 316 us
  waiting for transfers between devices  164 us (52%)
  starting transfers between devices  72.8 us (23%)
  matrix products  29 us (9%)
  other arithmetic  23.1 us (7%)
  between operations  14.4 us (5%)
  local copies, waits for them, and re-layouts  12.6 us (4%)
    all_gather x1, waiting for transfers between devices, per_device(): lax.all_gather(trace_values, ('row', 'gz'), axis=1, tiled=True)  56.3 us
    reduce_scatter x1, waiting for transfers between devices, per_device(): lax.psum_scatter(partial_flux, 'col', scatter_dimension=1, tiled=True)  53 us
    ppermute x9, waiting for transfers between devices, padded_2(): after = lax.ppermute(first, axis, down)  36.6 us
    ppermute x9, starting transfers between devices, padded_2(): before = lax.ppermute(last, axis, up)  31.7 us
    ppermute x9, starting transfers between devices, padded_2(): after = lax.ppermute(first, axis, down)  23.9 us
    all_to_all x1, starting transfers between devices, per_device(): lax.all_to_all(jnp.stack(jnp.split(surface_flux, lax.axis_size('gz'), axi...  17.1 us
    ppermute x9, waiting for transfers between devices, padded_2(): before = lax.ppermute(last, axis, up)  15.4 us
    dot_general x1, matrix products, per_device(): jnp.dot(owned_flux, placer, precision=lax.Precision.HIGHEST, preferred_el...  14.1 us
  transfers between devices with their start and end apart: 21, of which 14 were waited for; matrix products, arithmetic and copies ran while one was open for 7% of the time, Pallas kernels for 0%

profile of v1, /device:TPU:17, one launch (start us, length us, event | category | flops | bytes accessed | tf_op | source)
XLA Modules:
  0.0 315.6 jit_solution(11658105600428926654)
XLA Ops:
  7.2 8.3 %fusion.22 = bf16[128,1024]{1,0:T(8,128)(2,1)} fusion(bf16[16,8,64,128]{3,2,1,0:T(8,128)(2,1)} %bitcast.32, s32[1024]{0:T(1024)} %bitcast.34), kind=kOutput, calls=%fused_computation.46 | convolution fusion | flops 2156003328 | bytes 2363392 | tf_op jit(solution)/shard_map/dot_general | solution.py:44
  15.6 3.3 %copy.15 = bf16[128,8,8,128]{0,3,2,1:T(8,128)(2,1)S(1)} copy(bf16[128,8,8,128]{3,2,1,0:T(8,128)(2,1)} %param.6) | data formatting | bytes 4194304 | tf_op args[0]
  19.0 3.1 collective-permute-start
  24.0 4.2 %copy.16 = bf16[128,8,8,128]{0,3,2,1:T(8,128)(2,1)} copy(bf16[128,8,8,128]{3,2,1,0:T(8,128)(2,1)} %param.7) | data formatting | bytes 4194304 | tf_op args[1]
  31.8 3.5 %collective-permute-start.2 = (bf16[128,10,1,128]{0,3,2,1:T(8,128)(2,1)}, bf16[128,10,1,128]{0,3,2,1:T(8,128)(2,1)S(1)}, u32[]{:S(2)}, u32[]{:S(2)}) collective-permute-start(bf16[128,10,1,128]{0,3,2,1:T(8,128)(2,1)} %get-tuple-element.16), channel_id=1, source_target_pairs={{0,4},{4,8},{8,12},{12,16},{16,20},{20,24},{24,28},{28,32},{32,36}... | collective-permute-start | bytes 983048 | tf_op jit(solution)/shard_map/ppermute | solution.py:16
  35.4 4.5 %collective-permute-start.3 = (bf16[128,10,1,128]{0,3,2,1:T(8,128)(2,1)}, bf16[128,10,1,128]{0,3,2,1:T(8,128)(2,1)S(1)}, u32[]{:S(2)}, u32[]{:S(2)}) collective-permute-start(bf16[128,10,1,128]{0,3,2,1:T(8,128)(2,1)} %get-tuple-element.17), channel_id=1, source_target_pairs={{4,0},{8,4},{12,8},{16,12},{20,16},{24,20},{28,24},{32,28},{36,32}... | collective-permute-start | bytes 983048 | tf_op jit(solution)/shard_map/ppermute | solution.py:17
  39.9 56.3 %all-gather.2.cloned.1.call-done = bf16[128,16384]{1,0:T(8,128)(2,1)} async-done(((bf16[128,1024]{1,0:T(8,128)(2,1)}), bf16[128,16384]{1,0:T(8,128)(2,1)}) %all-gather.2.cloned.1.call-update) | async-done | bytes 4194320 | tf_op jit(solution)/shard_map/all_gather | solution.py:49
  96.2 6.7 %fusion.25 = f32[32,256]{0,1:T(8,128)} fusion(bf16[256,16384]{1,0:T(8,128)(2,1)} %param.9, bf16[128,16384]{1,0:T(8,128)(2,1)} %all-gather.2.cloned.1.call-done, s32[]{:T(128)S(6)} %select_n.3), kind=kOutput, calls=%fused_computation.47 | convolution fusion | flops 268435456 | bytes 9469956 | tf_op jit(solution)/shard_map/dot_general | solution.py:54
  107.4 53.0 %reduce-scatter.2.cloned.1.call-done = f32[32,16]{0,1:T(8,128)} async-done(((f32[32,256]{0,1:T(8,128)}), f32[32,16]{0,1:T(8,128)}) %reduce-scatter.2.cloned.1.call-update) | async-done | bytes 2064 | tf_op jit(solution)/shard_map/reduce_scatter | solution.py:57
  161.8 17.1 %all-to-all-start = ((f32[4,1,128]{2,1,0:T(1,128)}), f32[4,1,128]{2,1,0:T(1,128)}, u32[]{:S(2)}, u32[]{:S(2)}) async-start(f32[4,1,128]{2,1,0:T(1,128)} %reshape.42), calls=%async_computation.1 | async-start | bytes 4096 | tf_op jit(solution)/shard_map/all_to_all | solution.py:59
  179.0 4.8 %maximum_convert_fusion = f32[128,10,10,130]{0,3,2,1:T(8,128)} fusion(bf16[128,10,10,1]{0,3,2,1:T(2,128)(2,1)S(1)} %collective-permute-done.5, bf16[128,10,1,128]{0,3,2,1:T(8,128)(2,1)S(1)} %collective-permute-done.3, bf16[128,1,8,128]{0,3,2,1:T(8,128)(2,1)S(1)} %collective-permute-done.1, bf16[128,8,8,128]{0,3,2,1:T(8,128)(2,1)S(1)} %copy.15, ...), kind=kLoop, calls=%fused_computation.40 | loop fusion | flops 23296000 | bytes 9984000 | tf_op jit(solution)/shard_map/convert_element_type | solution.py:23
  188.2 14.1 %fusion.14 = (bf16[128,8,8,128]{0,3,2,1:T(8,128)(2,1)S(1)}, f32[128,8,8,128]{0,3,2,1:T(8,128)}) fusion(f32[128,10,10,130]{0,3,2,1:T(8,128)} %maximum_convert_fusion, bf16[128,8,8,128]{0,3,2,1:T(8,128)(2,1)S(1)} %copy.15, f32[8,8,128]{2,1,0:T(8,128)S(1)} %broadcast_add_fusion, s32[8,8,128]{2,1,0:T(8,128)S(1)} %copy-done.2, s32[4]{0:T(128)S(1)} %bitcast.35, ...), kind=kOutput, calls=%fused_computation.37 | convolution fusion | flops 66093056 | bytes 35719184 | tf_op jit(solution)/shard_map/dot_general | solution.py:66
  202.3 3.1 collective-permute-start.6
  206.7 3.8 %collective-permute-done.6 = bf16[128,1,8,128]{0,3,2,1:T(8,128)(2,1)S(1)} collective-permute-done((bf16[128,1,8,128]{0,3,2,1:T(8,128)(2,1)S(1)}, bf16[128,1,8,128]{0,3,2,1:T(8,128)(2,1)S(1)}, u32[]{:S(2)}, u32[]{:S(2)}) %collective-permute-start.6) | collective-permute-done | bytes 262176 | tf_op jit(solution)/shard_map/ppermute | solution.py:16
  210.5 3.8 %collective-permute-done.7 = bf16[128,1,8,128]{0,3,2,1:T(8,128)(2,1)S(1)} collective-permute-done((bf16[128,1,8,128]{0,3,2,1:T(8,128)(2,1)S(1)}, bf16[128,1,8,128]{0,3,2,1:T(8,128)(2,1)S(1)}, u32[]{:S(2)}, u32[]{:S(2)}) %collective-permute-start.7) | collective-permute-done | bytes 262176 | tf_op jit(solution)/shard_map/ppermute | solution.py:17
  214.4 2.9 collective-permute-start.8
  217.3 5.1 %collective-permute-start.9 = (bf16[128,10,1,128]{0,3,2,1:T(8,128)(2,1)S(1)}, bf16[128,10,1,128]{0,3,2,1:T(8,128)(2,1)S(1)}, u32[]{:S(2)}, u32[]{:S(2)}) collective-permute-start(bf16[128,10,1,128]{0,3,2,1:T(8,128)(2,1)S(1)} %get-tuple-element.15), channel_id=1, source_target_pairs={{4,0},{8,4},{12,8},{16,12},{20,16},{24,20},{28,24},{32,28},{36,32}... | collective-permute-start | bytes 983048 | tf_op jit(solution)/shard_map/ppermute | solution.py:17
  222.4 4.2 %collective-permute-done.8 = bf16[128,10,1,128]{0,3,2,1:T(8,128)(2,1)S(1)} collective-permute-done((bf16[128,10,1,128]{0,3,2,1:T(8,128)(2,1)S(1)}, bf16[128,10,1,128]{0,3,2,1:T(8,128)(2,1)S(1)}, u32[]{:S(2)}, u32[]{:S(2)}) %collective-permute-start.8) | collective-permute-done | bytes 327712 | tf_op jit(solution)/shard_map/ppermute | solution.py:16
  226.7 7.3 %collective-permute-done.9 = bf16[128,10,1,128]{0,3,2,1:T(8,128)(2,1)S(1)} collective-permute-done((bf16[128,10,1,128]{0,3,2,1:T(8,128)(2,1)S(1)}, bf16[128,10,1,128]{0,3,2,1:T(8,128)(2,1)S(1)}, u32[]{:S(2)}, u32[]{:S(2)}) %collective-permute-start.9) | collective-permute-done | bytes 327712 | tf_op jit(solution)/shard_map/ppermute | solution.py:17
  234.1 7.6 %collective-permute-start.10 = (bf16[128,10,10,1]{0,3,2,1:T(2,128)(2,1)S(1)}, bf16[128,10,10,1]{0,3,2,1:T(2,128)(2,1)S(1)}, u32[]{:S(2)}, u32[]{:S(2)}) collective-permute-start(bf16[128,10,10,1]{0,3,2,1:T(2,128)(2,1)S(1)} %get-tuple-element.8), channel_id=1, source_target_pairs={{0,1},{1,2},{2,3},{4,5},{5,6},{6,7},{8,9},{9,10},{10,11},{12,13},{... | collective-permute-start | bytes 76808 | tf_op jit(solution)/shard_map/ppermute | solution.py:16
  243.9 7.4 %collective-permute-done.11 = bf16[128,10,10,1]{0,3,2,1:T(2,128)(2,1)S(1)} collective-permute-done((bf16[128,10,10,1]{0,3,2,1:T(2,128)(2,1)S(1)}, bf16[128,10,10,1]{0,3,2,1:T(2,128)(2,1)S(1)}, u32[]{:S(2)}, u32[]{:S(2)}) %collective-permute-start.11) | collective-permute-done | bytes 25632 | tf_op jit(solution)/shard_map/ppermute | solution.py:17
  251.3 3.0 maximum_convert_fusion.1
  254.3 4.5 %fusion.15 = bf16[128,8,8,128]{0,3,2,1:T(8,128)(2,1)S(1)} fusion(f32[128,8,8,128]{0,3,2,1:T(8,128)S(1)} %copy-done, f32[128,10,10,130]{0,3,2,1:T(8,128)S(1)} %maximum_convert_fusion.1, bf16[128,8,8,128]{0,3,2,1:T(8,128)(2,1)S(1)} %get-tuple-element.28, f32[8,8,128]{2,1,0:T(8,128)S(1)} %broadcast_add_fusion), kind=kLoop, calls=%fused_computation.38 | loop fusion | flops 13631488 | bytes 33587200 | tf_op jit(solution)/shard_map/convert_element_type | solution.py:28
  258.9 3.1 collective-permute-start.12
  265.3 3.8 %collective-permute-done.13 = bf16[128,1,8,128]{0,3,2,1:T(8,128)(2,1)S(1)} collective-permute-done((bf16[128,1,8,128]{0,3,2,1:T(8,128)(2,1)S(1)}, bf16[128,1,8,128]{0,3,2,1:T(8,128)(2,1)S(1)}, u32[]{:S(2)}, u32[]{:S(2)}) %collective-permute-start.13) | collective-permute-done | bytes 262176 | tf_op jit(solution)/shard_map/ppermute | solution.py:17
  269.2 4.6 %collective-permute-start.14 = (bf16[128,10,1,128]{0,3,2,1:T(8,128)(2,1)S(1)}, bf16[128,10,1,128]{0,3,2,1:T(8,128)(2,1)S(1)}, u32[]{:S(2)}, u32[]{:S(2)}) collective-permute-start(bf16[128,10,1,128]{0,3,2,1:T(8,128)(2,1)S(1)} %get-tuple-element.12), channel_id=1, source_target_pairs={{0,4},{4,8},{8,12},{12,16},{16,20},{20,24},{24,28},{28,32},{32,36}... | collective-permute-start | bytes 983048 | tf_op jit(solution)/shard_map/ppermute | solution.py:16
  273.8 3.4 %collective-permute-start.15 = (bf16[128,10,1,128]{0,3,2,1:T(8,128)(2,1)S(1)}, bf16[128,10,1,128]{0,3,2,1:T(8,128)(2,1)S(1)}, u32[]{:S(2)}, u32[]{:S(2)}) collective-permute-start(bf16[128,10,1,128]{0,3,2,1:T(8,128)(2,1)S(1)} %get-tuple-element.13), channel_id=1, source_target_pairs={{4,0},{8,4},{12,8},{16,12},{20,16},{24,20},{28,24},{32,28},{36,32}... | collective-permute-start | bytes 983048 | tf_op jit(solution)/shard_map/ppermute | solution.py:17
  277.2 5.4 %collective-permute-done.14 = bf16[128,10,1,128]{0,3,2,1:T(8,128)(2,1)S(1)} collective-permute-done((bf16[128,10,1,128]{0,3,2,1:T(8,128)(2,1)S(1)}, bf16[128,10,1,128]{0,3,2,1:T(8,128)(2,1)S(1)}, u32[]{:S(2)}, u32[]{:S(2)}) %collective-permute-start.14) | collective-permute-done | bytes 327712 | tf_op jit(solution)/shard_map/ppermute | solution.py:16
  282.6 4.6 %collective-permute-done.15 = bf16[128,10,1,128]{0,3,2,1:T(8,128)(2,1)S(1)} collective-permute-done((bf16[128,10,1,128]{0,3,2,1:T(8,128)(2,1)S(1)}, bf16[128,10,1,128]{0,3,2,1:T(8,128)(2,1)S(1)}, u32[]{:S(2)}, u32[]{:S(2)}) %collective-permute-start.15) | collective-permute-done | bytes 327712 | tf_op jit(solution)/shard_map/ppermute | solution.py:17
  291.6 6.9 %collective-permute-done.17 = bf16[128,10,10,1]{0,3,2,1:T(2,128)(2,1)S(1)} collective-permute-done((bf16[128,10,10,1]{0,3,2,1:T(2,128)(2,1)S(1)}, bf16[128,10,10,1]{0,3,2,1:T(2,128)(2,1)S(1)}, u32[]{:S(2)}, u32[]{:S(2)}) %collective-permute-start.17) | collective-permute-done | bytes 25632 | tf_op jit(solution)/shard_map/ppermute | solution.py:17
  298.5 3.0 maximum_convert_fusion.2
  301.4 4.5 %fusion.16 = bf16[128,8,8,128]{0,3,2,1:T(8,128)(2,1)S(1)} fusion(f32[128,8,8,128]{0,3,2,1:T(8,128)S(1)} %copy-done, f32[128,10,10,130]{0,3,2,1:T(8,128)S(1)} %maximum_convert_fusion.2, bf16[128,8,8,128]{0,3,2,1:T(8,128)(2,1)S(1)} %fusion.15, f32[8,8,128]{2,1,0:T(8,128)S(1)} %broadcast_add_fusion), kind=kLoop, calls=%fused_computation.39 | loop fusion | flops 13631488 | bytes 33587200 | tf_op jit(solution)/shard_map/convert_element_type | solution.py:28
  (50 shorter events, 30.3 us)
Async XLA Ops:
  7.2 89.1 %all-gather.2.cloned.1.call-start = ((), (), s32[]{:S(2)}) async-start(), calls=%async_computation.2 | async-start | bytes 4456448 | tf_op jit(solution)/shard_map/all_gather | solution.py:49
  15.5 12.7 %copy-start.1 = (f32[8,8,128]{2,1,0:T(8,128)S(1)}, f32[8,8,128]{2,1,0:T(8,128)}, u32[]{:S(2)}) copy-start(f32[8,8,128]{2,1,0:T(8,128)} %param.8) | copy-start | bytes 98308
  15.5 144.8 %reduce-scatter.2.cloned.1.call-start = ((), (), s32[]{:S(2)}) async-start(), calls=%async_computation.3 | async-start | bytes 139264 | tf_op jit(solution)/shard_map/reduce_scatter | solution.py:57
  19.0 9.2 %collective-permute-start = (bf16[128,1,8,128]{0,3,2,1:T(8,128)(2,1)S(1)}, bf16[128,1,8,128]{0,3,2,1:T(8,128)(2,1)S(1)}, u32[]{:S(2)}, u32[]{:S(2)}) collective-permute-start(bf16[128,1,8,128]{0,3,2,1:T(8,128)(2,1)S(1)} %get-tuple-element.22), channel_id=1, source_target_pairs={{0,64},{64,128},{128,192},{1,65},{65,129},{129,193},{2,66},{66,130... | collective-permute-start | bytes 786440 | tf_op jit(solution)/shard_map/ppermute | solution.py:16
  22.1 8.8 %collective-permute-start.1 = (bf16[128,1,8,128]{0,3,2,1:T(8,128)(2,1)S(1)}, bf16[128,1,8,128]{0,3,2,1:T(8,128)(2,1)S(1)}, u32[]{:S(2)}, u32[]{:S(2)}) collective-permute-start(bf16[128,1,8,128]{0,3,2,1:T(8,128)(2,1)S(1)} %get-tuple-element.23), channel_id=1, source_target_pairs={{64,0},{128,64},{192,128},{65,1},{129,65},{193,129},{66,2},{130,66... | collective-permute-start | bytes 786440 | tf_op jit(solution)/shard_map/ppermute | solution.py:17
  31.8 71.1 %collective-permute-start.2 = (bf16[128,10,1,128]{0,3,2,1:T(8,128)(2,1)}, bf16[128,10,1,128]{0,3,2,1:T(8,128)(2,1)S(1)}, u32[]{:S(2)}, u32[]{:S(2)}) collective-permute-start(bf16[128,10,1,128]{0,3,2,1:T(8,128)(2,1)} %get-tuple-element.16), channel_id=1, source_target_pairs={{0,4},{4,8},{8,12},{12,16},{16,20},{20,24},{24,28},{28,32},{32,36}... | collective-permute-start | bytes 983048 | tf_op jit(solution)/shard_map/ppermute | solution.py:16
  35.4 67.6 %collective-permute-start.3 = (bf16[128,10,1,128]{0,3,2,1:T(8,128)(2,1)}, bf16[128,10,1,128]{0,3,2,1:T(8,128)(2,1)S(1)}, u32[]{:S(2)}, u32[]{:S(2)}) collective-permute-start(bf16[128,10,1,128]{0,3,2,1:T(8,128)(2,1)} %get-tuple-element.17), channel_id=1, source_target_pairs={{4,0},{8,4},{12,8},{16,12},{20,16},{24,20},{28,24},{32,28},{36,32}... | collective-permute-start | bytes 983048 | tf_op jit(solution)/shard_map/ppermute | solution.py:17
  103.1 75.9 %collective-permute-start.4 = (bf16[128,10,10,1]{0,3,2,1:T(2,128)(2,1)S(1)}, bf16[128,10,10,1]{0,3,2,1:T(2,128)(2,1)S(1)}, u32[]{:S(2)}, u32[]{:S(2)}) collective-permute-start(bf16[128,10,10,1]{0,3,2,1:T(2,128)(2,1)S(1)} %get-tuple-element.10), channel_id=1, source_target_pairs={{0,1},{1,2},{2,3},{4,5},{5,6},{6,7},{8,9},{9,10},{10,11},{12,13},{... | collective-permute-start | bytes 76808 | tf_op jit(solution)/shard_map/ppermute | solution.py:16
  105.0 74.0 %collective-permute-start.5 = (bf16[128,10,10,1]{0,3,2,1:T(2,128)(2,1)S(1)}, bf16[128,10,10,1]{0,3,2,1:T(2,128)(2,1)S(1)}, u32[]{:S(2)}, u32[]{:S(2)}) collective-permute-start(bf16[128,10,10,1]{0,3,2,1:T(2,128)(2,1)S(1)} %get-tuple-element.11), channel_id=1, source_target_pairs={{1,0},{2,1},{3,2},{5,4},{6,5},{7,6},{9,8},{10,9},{11,10},{13,12},{... | collective-permute-start | bytes 76808 | tf_op jit(solution)/shard_map/ppermute | solution.py:17
  161.8 24.2 %all-to-all-start = ((f32[4,1,128]{2,1,0:T(1,128)}), f32[4,1,128]{2,1,0:T(1,128)}, u32[]{:S(2)}, u32[]{:S(2)}) async-start(f32[4,1,128]{2,1,0:T(1,128)} %reshape.42), calls=%async_computation.1 | async-start | bytes 4096 | tf_op jit(solution)/shard_map/all_to_all | solution.py:59
  179.0 9.2 %copy-start.2 = (s32[8,8,128]{2,1,0:T(8,128)S(1)}, s32[8,8,128]{2,1,0:T(8,128)}, u32[]{:S(2)}) copy-start(s32[8,8,128]{2,1,0:T(8,128)} %multiply_add_fusion) | copy-start | bytes 98308
  179.0 9.2 %copy-start.3 = (s32[1,1,1,4]{3,2,1,0:T(1,128)S(1)}, s32[1,1,1,4]{3,2,1,0:T(1,128)}, u32[]{:S(2)}) copy-start(s32[1,1,1,4]{3,2,1,0:T(1,128)} %param.11) | copy-start | bytes 52
  202.3 8.2 %collective-permute-start.6 = (bf16[128,1,8,128]{0,3,2,1:T(8,128)(2,1)S(1)}, bf16[128,1,8,128]{0,3,2,1:T(8,128)(2,1)S(1)}, u32[]{:S(2)}, u32[]{:S(2)}) collective-permute-start(bf16[128,1,8,128]{0,3,2,1:T(8,128)(2,1)S(1)} %get-tuple-element.20), channel_id=1, source_target_pairs={{0,64},{64,128},{128,192},{1,65},{65,129},{129,193},{2,66},{66,130... | collective-permute-start | bytes 786440 | tf_op jit(solution)/shard_map/ppermute | solution.py:16
  205.4 8.9 %collective-permute-start.7 = (bf16[128,1,8,128]{0,3,2,1:T(8,128)(2,1)S(1)}, bf16[128,1,8,128]{0,3,2,1:T(8,128)(2,1)S(1)}, u32[]{:S(2)}, u32[]{:S(2)}) collective-permute-start(bf16[128,1,8,128]{0,3,2,1:T(8,128)(2,1)S(1)} %get-tuple-element.21), channel_id=1, source_target_pairs={{64,0},{128,64},{192,128},{65,1},{129,65},{193,129},{66,2},{130,66... | collective-permute-start | bytes 786440 | tf_op jit(solution)/shard_map/ppermute | solution.py:17
  214.4 12.2 %collective-permute-start.8 = (bf16[128,10,1,128]{0,3,2,1:T(8,128)(2,1)S(1)}, bf16[128,10,1,128]{0,3,2,1:T(8,128)(2,1)S(1)}, u32[]{:S(2)}, u32[]{:S(2)}) collective-permute-start(bf16[128,10,1,128]{0,3,2,1:T(8,128)(2,1)S(1)} %get-tuple-element.14), channel_id=1, source_target_pairs={{0,4},{4,8},{8,12},{12,16},{16,20},{20,24},{24,28},{28,32},{32,36}... | collective-permute-start | bytes 983048 | tf_op jit(solution)/shard_map/ppermute | solution.py:16
  217.3 16.7 %collective-permute-start.9 = (bf16[128,10,1,128]{0,3,2,1:T(8,128)(2,1)S(1)}, bf16[128,10,1,128]{0,3,2,1:T(8,128)(2,1)S(1)}, u32[]{:S(2)}, u32[]{:S(2)}) collective-permute-start(bf16[128,10,1,128]{0,3,2,1:T(8,128)(2,1)S(1)} %get-tuple-element.15), channel_id=1, source_target_pairs={{4,0},{8,4},{12,8},{16,12},{20,16},{24,20},{28,24},{32,28},{36,32}... | collective-permute-start | bytes 983048 | tf_op jit(solution)/shard_map/ppermute | solution.py:17
  234.1 9.8 %collective-permute-start.10 = (bf16[128,10,10,1]{0,3,2,1:T(2,128)(2,1)S(1)}, bf16[128,10,10,1]{0,3,2,1:T(2,128)(2,1)S(1)}, u32[]{:S(2)}, u32[]{:S(2)}) collective-permute-start(bf16[128,10,10,1]{0,3,2,1:T(2,128)(2,1)S(1)} %get-tuple-element.8), channel_id=1, source_target_pairs={{0,1},{1,2},{2,3},{4,5},{5,6},{6,7},{8,9},{9,10},{10,11},{12,13},{... | collective-permute-start | bytes 76808 | tf_op jit(solution)/shard_map/ppermute | solution.py:16
  241.7 12.6 %copy-start = (f32[128,8,8,128]{0,3,2,1:T(8,128)S(1)}, f32[128,8,8,128]{0,3,2,1:T(8,128)}, u32[]{:S(2)}) copy-start(f32[128,8,8,128]{0,3,2,1:T(8,128)} %get-tuple-element.29) | copy-start | bytes 12582916
  241.7 9.6 %collective-permute-start.11 = (bf16[128,10,10,1]{0,3,2,1:T(2,128)(2,1)S(1)}, bf16[128,10,10,1]{0,3,2,1:T(2,128)(2,1)S(1)}, u32[]{:S(2)}, u32[]{:S(2)}) collective-permute-start(bf16[128,10,10,1]{0,3,2,1:T(2,128)(2,1)S(1)} %get-tuple-element.9), channel_id=1, source_target_pairs={{1,0},{2,1},{3,2},{5,4},{6,5},{7,6},{9,8},{10,9},{11,10},{13,12},{... | collective-permute-start | bytes 76808 | tf_op jit(solution)/shard_map/ppermute | solution.py:17
  258.9 6.4 %collective-permute-start.12 = (bf16[128,1,8,128]{0,3,2,1:T(8,128)(2,1)S(1)}, bf16[128,1,8,128]{0,3,2,1:T(8,128)(2,1)S(1)}, u32[]{:S(2)}, u32[]{:S(2)}) collective-permute-start(bf16[128,1,8,128]{0,3,2,1:T(8,128)(2,1)S(1)} %get-tuple-element.18), channel_id=1, source_target_pairs={{0,64},{64,128},{128,192},{1,65},{65,129},{129,193},{2,66},{66,130... | collective-permute-start | bytes 786440 | tf_op jit(solution)/shard_map/ppermute | solution.py:16
  262.0 7.1 %collective-permute-start.13 = (bf16[128,1,8,128]{0,3,2,1:T(8,128)(2,1)S(1)}, bf16[128,1,8,128]{0,3,2,1:T(8,128)(2,1)S(1)}, u32[]{:S(2)}, u32[]{:S(2)}) collective-permute-start(bf16[128,1,8,128]{0,3,2,1:T(8,128)(2,1)S(1)} %get-tuple-element.19), channel_id=1, source_target_pairs={{64,0},{128,64},{192,128},{65,1},{129,65},{193,129},{66,2},{130,66... | collective-permute-start | bytes 786440 | tf_op jit(solution)/shard_map/ppermute | solution.py:17
  269.2 13.4 %collective-permute-start.14 = (bf16[128,10,1,128]{0,3,2,1:T(8,128)(2,1)S(1)}, bf16[128,10,1,128]{0,3,2,1:T(8,128)(2,1)S(1)}, u32[]{:S(2)}, u32[]{:S(2)}) collective-permute-start(bf16[128,10,1,128]{0,3,2,1:T(8,128)(2,1)S(1)} %get-tuple-element.12), channel_id=1, source_target_pairs={{0,4},{4,8},{8,12},{12,16},{16,20},{20,24},{24,28},{28,32},{32,36}... | collective-permute-start | bytes 983048 | tf_op jit(solution)/shard_map/ppermute | solution.py:16
  273.8 13.4 %collective-permute-start.15 = (bf16[128,10,1,128]{0,3,2,1:T(8,128)(2,1)S(1)}, bf16[128,10,1,128]{0,3,2,1:T(8,128)(2,1)S(1)}, u32[]{:S(2)}, u32[]{:S(2)}) collective-permute-start(bf16[128,10,1,128]{0,3,2,1:T(8,128)(2,1)S(1)} %get-tuple-element.13), channel_id=1, source_target_pairs={{4,0},{8,4},{12,8},{16,12},{20,16},{24,20},{28,24},{32,28},{36,32}... | collective-permute-start | bytes 983048 | tf_op jit(solution)/shard_map/ppermute | solution.py:17
  287.2 4.3 %collective-permute-start.16 = (bf16[128,10,10,1]{0,3,2,1:T(2,128)(2,1)S(1)}, bf16[128,10,10,1]{0,3,2,1:T(2,128)(2,1)S(1)}, u32[]{:S(2)}, u32[]{:S(2)}) collective-permute-start(bf16[128,10,10,1]{0,3,2,1:T(2,128)(2,1)S(1)} %get-tuple-element.6), channel_id=1, source_target_pairs={{0,1},{1,2},{2,3},{4,5},{5,6},{6,7},{8,9},{9,10},{10,11},{12,13},{... | collective-permute-start | bytes 76808 | tf_op jit(solution)/shard_map/ppermute | solution.py:16
  289.1 9.3 %collective-permute-start.17 = (bf16[128,10,10,1]{0,3,2,1:T(2,128)(2,1)S(1)}, bf16[128,10,10,1]{0,3,2,1:T(2,128)(2,1)S(1)}, u32[]{:S(2)}, u32[]{:S(2)}) collective-permute-start(bf16[128,10,10,1]{0,3,2,1:T(2,128)(2,1)S(1)} %get-tuple-element.7), channel_id=1, source_target_pairs={{1,0},{2,1},{3,2},{5,4},{6,5},{7,6},{9,8},{10,9},{11,10},{13,12},{... | collective-permute-start | bytes 76808 | tf_op jit(solution)/shard_map/ppermute | solution.py:17
Sparse Core Ops, SparseCore 0:
  15.7 80.5 all-gather.1
  103.1 57.2 reduce-scatter.1
